TPU v7x, 32 devices: a whole 2x2x4 slice. The times are simulated.
32 devices in a mesh: group: 8 (over z, y), lat: 2 (over x), rad: 2 (over core).
Axes of the slice: x: 2, y: 2, z: 4, core: 2. Of those that a mesh axis runs over, the one named last changes fastest.
Arguments:
- displacement_prev: float32 [3, 4, 128, 256], P(None, 'rad', 'group', 'lat'), may hold values from -2.5 to 2.5
- shear_modulus: float32 [4, 128, 256], P('rad', 'group', 'lat'), may hold values from 1 to 10
- viscosity: float32 [4, 128, 256], P('rad', 'group', 'lat'), may hold values from 0.5 to 20
- element_matrix: float32 [24, 24], replicated, as said below
- regrid_index: int32 [128, 2, 4], P('group', 'lat'), may hold values from 0 to 63
- regrid_weight: float32 [128, 2, 4], P('group', 'lat'), may hold values from 0.1 to 0.6
- ice_thickness: float32 [32, 256], P('lat'), may hold values from 0.5 to 4
- bed_elevation: float32 [32, 256], P('lat'), may hold values from -3 to 3
- basal_friction: float32 [32, 256], P('lat'), may hold values from 0.2 to 5
- ice_mask: int32 [32, 256], P('lat'), may hold values 0 or 1
- speed_guess: float32 [16, 32, 256], P(None, 'lat'), may hold values from -3 to 3
Outputs:
- displacement: float32 [3, 4, 128, 256], P(None, 'rad', 'group', 'lat')
- bed_new: float32 [32, 256], P('lat')
Inputs may be any that keep to these rules, and one draw needn't show every extreme that they name: `regrid_index`: names a block of the ice map: block b is row b // 2, columns 128 * (b % 2) to 128 * (b % 2) + 127. `element_matrix`: symmetric positive definite.
All inputs are finite; a program needn't handle non-finite values. No bound on the sum of `ice_mask` on one device may be relied on, other than what follows from the above.
Results may differ from a plain program's by a relative error of at most 0.0019.
Values may be sent and summed in bfloat16 or wider, within the bound.
No kernel may reach another device: no remote copies, remote signals or barrier semaphores. Data moves between devices by JAX's collectives and lax.ppermute only.
A program may use at most 64 MiB of HBM per device.

v0:
```python
import jax
import jax.numpy as jnp
from jax import lax
from jax.sharding import PartitionSpec as P

BLOCK = 128
SWEEPS = 6
ITERS = 4
LOAD_SCALE = 20.0
UPLIFT_SCALE = 0.5
TIME_SCALE = 1.0
ICE_STEP = 0.5
ASPECT = 0.01
STRAIN_FLOOR = 0.01
CORNERS = [
    (layer_bit, row_bit, col_bit)
    for layer_bit in (0, 1)
    for row_bit in (0, 1)
    for col_bit in (0, 1)
]


def padded(cells, sides, width):
    for axis, dim in sides:
        count = lax.axis_size(axis)
        ends = count - 1
        head = lax.slice_in_dim(cells, 0, width, axis=dim)
        tail = lax.slice_in_dim(cells, cells.shape[dim] - width, cells.shape[dim], axis=dim)
        cells = jnp.concatenate(
            [
                lax.ppermute(tail, axis, [(i, (i + 1) % count) for i in range(ends)]),
                cells,
                lax.ppermute(head, axis, [((i + 1) % count, i) for i in range(ends)]),
            ],
            axis=dim,
        )
    return cells


def broadcast(value, axis, source):
    kept = jnp.where(lax.axis_index(axis) == source, value, 0).astype(value.dtype)
    return lax.psum(kept, axis)


def corner_mean(padded_coef):
    layer_count = padded_coef.shape[0] - 1
    col_count = padded_coef.shape[1] - 1
    depth_count = padded_coef.shape[2] - 1
    summed = jnp.zeros((layer_count, col_count, depth_count), jnp.float32)
    for layer_bit, row_bit, col_bit in CORNERS:
        summed = (
            summed
            + padded_coef[
                layer_bit : layer_bit + layer_count,
                row_bit : row_bit + col_count,
                col_bit : col_bit + depth_count,
            ]
        )
    return summed / 8.0


def element_apply(padded_field, element_coef, kernel):
    layer_count, col_count, depth_count = element_coef.shape
    pieces = [
        padded_field[
            :,
            layer_bit : layer_bit + layer_count,
            row_bit : row_bit + col_count,
            col_bit : col_bit + depth_count,
        ]
        for layer_bit, row_bit, col_bit in CORNERS
    ]
    stacked = jnp.concatenate(pieces, 0)
    forces = (
        jnp.einsum("pq,qrab->prab", kernel, stacked, precision=lax.Precision.HIGHEST) * element_coef
    )
    summed = jnp.zeros((3, layer_count - 1, col_count - 1, depth_count - 1), jnp.float32)
    for corner_id, (layer_bit, row_bit, col_bit) in enumerate(CORNERS):
        summed = (
            summed
            + forces[
                3 * corner_id : 3 * corner_id + 3,
                1 - layer_bit : layer_count - layer_bit,
                1 - row_bit : col_count - row_bit,
                1 - col_bit : depth_count - col_bit,
            ]
        )
    return summed


def column_neighbours(values):
    zero_col = jnp.zeros_like(values[..., :1])
    east_side = jnp.concatenate([values[..., 1:], zero_col], -1)
    west_side = jnp.concatenate([zero_col, values[..., :-1]], -1)
    return (east_side, west_side)


def ice_sweep(velocity, padded_speed, thickness, friction, driving):
    levels = velocity.shape[0]
    north_side = padded_speed[:, 2:, :]
    south_side = padded_speed[:, :-2, :]
    east_side, west_side = column_neighbours(velocity)
    inverse = (levels - 1) / thickness
    slope_rows = 0.5 * (north_side - south_side)
    slope_cols = 0.5 * (east_side - west_side)
    slope_levels = (
        jnp.concatenate(
            [
                velocity[1:2] - velocity[0:1],
                0.5 * (velocity[2:] - velocity[:-2]),
                velocity[-1:] - velocity[-2:-1],
            ],
            0,
        )
        * inverse
    )
    strain = slope_rows**2 + 0.25 * slope_cols**2 + 0.25 * slope_levels**2 + STRAIN_FLOOR
    stiffness = 0.5 * strain ** (-1.0 / 3.0)
    vertical = ASPECT * inverse**2 * 0.5 * (stiffness[1:] + stiffness[:-1])
    neighbours = stiffness * (north_side + south_side + east_side + west_side)
    factors = []
    upper_prev = None
    values_prev = None
    for level_id in range(levels):
        diagonal = 4.0 * stiffness[level_id]
        if level_id > 0:
            diagonal = diagonal + vertical[level_id - 1]
        if level_id < levels - 1:
            diagonal = diagonal + vertical[level_id]
        if level_id == 0:
            diagonal = diagonal + friction
        right_side = driving + neighbours[level_id]
        if level_id > 0:
            lower_coef = -vertical[level_id - 1]
            diagonal = diagonal - lower_coef * upper_prev
            right_side = right_side - lower_coef * values_prev
        upper_prev = -vertical[level_id] / diagonal if level_id < levels - 1 else None
        values_prev = right_side / diagonal
        factors.append((upper_prev, values_prev))
    solution = [None] * levels
    solution[levels - 1] = factors[levels - 1][1]
    for level_id in range(levels - 2, -1, -1):
        solution[level_id] = factors[level_id][1] - factors[level_id][0] * solution[level_id + 1]
    return jnp.stack(solution, 0)


def ice_tile_load(is_ice, ice_thickness, bed_elevation, basal_friction, ice_mask, speed_guess):
    ice_present = ice_mask.astype(jnp.float32)
    surface = bed_elevation + ice_thickness
    padded_surface = padded(surface, (("lat", 0),), 1)
    driving = -ice_present * ice_thickness * 0.5 * (padded_surface[2:] - padded_surface[:-2])
    velocity = speed_guess
    for sweep_id in range(SWEEPS):
        padded_speed = padded(velocity, (("lat", 1),), 1)

        def run_sweep(operands):
            return ice_sweep(operands[0], operands[1], ice_thickness, basal_friction, driving)

        def keep_speed(operands):
            return operands[0]

        velocity = lax.cond(is_ice, run_sweep, keep_speed, (velocity, padded_speed))
    ice_flux = ice_thickness * jnp.mean(velocity, 0)
    padded_flux = padded(ice_flux, (("lat", 0),), 1)
    new_thickness = ice_thickness - ICE_STEP * 0.5 * (padded_flux[2:] - padded_flux[:-2])
    ice_load = (ice_present * new_thickness).astype(jnp.bfloat16)
    return jnp.where(is_ice, ice_load, jnp.zeros_like(ice_load))


def per_device(
    displacement_prev,
    shear_modulus,
    viscosity,
    element_matrix,
    regrid_index,
    regrid_weight,
    ice_thickness,
    bed_elevation,
    basal_friction,
    ice_mask,
    speed_guess,
):
    ice_root = lax.axis_size("group") - 1
    is_ice = lax.axis_index("group") == ice_root
    shell_group = (lax.axis_index("group") < ice_root).astype(jnp.float32)
    top_core = (lax.axis_index("rad") == 0).astype(jnp.float32)
    relax_ratio = TIME_SCALE * shear_modulus / viscosity
    modulus = shell_group * shear_modulus / (1.0 + relax_ratio)
    relaxed = modulus * relax_ratio / (1.0 + relax_ratio)
    start_field = displacement_prev * shell_group
    joined = jnp.concatenate([start_field, modulus[None], relaxed[None]], 0)
    padded_all = padded(joined, (("group", 2), ("lat", 3), ("rad", 1)), 1)
    coef_main = corner_mean(padded_all[3])
    coef_relax = corner_mean(padded_all[4])
    ice_load = ice_tile_load(
        is_ice, ice_thickness, bed_elevation, basal_friction, ice_mask, speed_guess
    )

    def skip_shell(unused):
        return jnp.zeros(start_field.shape, jnp.float32)

    def shell_branch(unused):
        return element_apply(padded_all[:3], coef_relax, element_matrix) * shell_group

    relax_force = lax.cond(is_ice, skip_shell, shell_branch, 0)
    shell_tile = broadcast(ice_load, "group", ice_root)
    ice_field = lax.all_gather(shell_tile, "lat", axis=0, tiled=True)
    row_count = regrid_index.shape[0]
    flat_index = regrid_index.reshape(-1)
    weights = regrid_weight.reshape(row_count, -1)
    blocks = ice_field.reshape(-1, BLOCK)
    picked = jnp.take(blocks, flat_index, axis=0).astype(jnp.float32).reshape(row_count, -1, BLOCK)
    surface_thickness = jnp.sum(weights[..., None] * picked, 1)
    load_field = (
        jnp.zeros(start_field.shape, jnp.float32)
        .at[2, 0]
        .set(-LOAD_SCALE * surface_thickness * top_core * shell_group)
    )
    residual = load_field - relax_force

    def global_norm(values):
        return lax.psum(jnp.sum(values * values), ("group", "lat", "rad"))

    solution = start_field
    direction = residual
    norm_now = global_norm(residual)
    for iter_id in range(ITERS):
        padded_field = padded(direction, (("group", 2), ("lat", 3), ("rad", 1)), 1)
        mapped = element_apply(padded_field, coef_main, element_matrix) * shell_group
        step_size = norm_now / lax.psum(jnp.sum(direction * mapped), ("group", "lat", "rad"))
        solution = solution + step_size * direction
        residual = residual - step_size * mapped
        norm_next = global_norm(residual)
        direction = residual + norm_next / norm_now * direction
        norm_now = norm_next
    layer_total = solution.shape[1] * lax.axis_size("rad")
    surface_lift = jnp.sum(solution[2], 0) / layer_total
    contrib = (weights[..., None] * surface_lift[:, None, :]).reshape(-1, BLOCK)
    tile_height = 2 * ice_thickness.shape[0]
    targets = lax.broadcasted_iota(
        jnp.int32, (tile_height * lax.axis_size("lat"), flat_index.shape[0]), 0
    )
    selector = (targets == flat_index[None, :]).astype(jnp.float32)
    all_lift = lax.psum(
        jnp.dot(
            selector, contrib, precision=lax.Precision.HIGHEST, preferred_element_type=jnp.float32
        ),
        ("group", "lat", "rad"),
    )
    own_lift = lax.dynamic_slice_in_dim(
        all_lift, lax.axis_index("lat") * tile_height, tile_height, 0
    )
    bed_new = bed_elevation + UPLIFT_SCALE * own_lift.reshape(bed_elevation.shape)
    return (solution, bed_new)


def solution(mesh):
    in_specs = (
        P(None, "rad", "group", "lat"),
        P("rad", "group", "lat"),
        P("rad", "group", "lat"),
        P(),
        P("group", "lat", None),
        P("group", "lat", None),
        P("lat", None),
        P("lat", None),
        P("lat", None),
        P("lat", None),
        P(None, "lat", None),
    )
    out_specs = (P(None, "rad", "group", "lat"), P("lat", None))
    return jax.shard_map(
        per_device, mesh=mesh, in_specs=in_specs, out_specs=out_specs, check_vma=False
    )
```

profile of v0, /device:TPU:0, one launch (start us, length us, event | category | flops | bytes accessed | tf_op | source)
XLA Modules:
  0.0 650.5 jit_solution(13611516230514924410)
XLA Ops:
  5.3 5.5 collective-permute-start.16
  30.6 4.5 collective-permute-start.4
  40.4 4.5 collective-permute-start.6
  49.7 4.5 collective-permute-start.8
  55.7 4.6 collective-permute-start.18
  63.6 4.5 collective-permute-start.10
  89.9 7.3 %conditional.13 = (f32[3,2,16,128]{3,0,2,1:T(4,128)S(1)}) conditional(s32[]{:T(128)} %convert_element_type.28, (f32[5,4,18,130]{3,0,2,1:T(8,128)S(1)}, f32[24,24]{1,0:T(8,128)S(1)}, f32[3,17,129]{2,0,1:T(4,128)}, f32[]{:T(128)}) %tuple.375, () %tuple.72), branch_computations={%region_15.16_spmd, %region_16.17_spmd} | conditional | flops 45782880 | bytes 5078236 | solution.py:205
  98.1 87.5 %psum.70 = bf16[16,256]{1,0:T(8,128)(2,1)S(1)} all-reduce(bf16[16,256]{1,0:T(8,128)(2,1)S(1)} %select_select_fusion), channel_id=1, replica_groups=mesh['group'=8,'lat'=2,'rad'=2] {'group'}, use_global_device_ids=true, to_apply=%region_13.14 | all-reduce | flops 4096 | bytes 16384 | tf_op jit(solution)/shard_map/psum | solution.py:42
  192.9 4.5 collective-permute-start.22
  200.2 4.5 collective-permute-start.24
  219.4 40.3 %all-reduce.13 = (f32[]{:T(128)}, f32[]{:T(128)}) all-reduce(f32[]{:T(128)} %get-tuple-element.190, f32[]{:T(128)} %get-tuple-element.189), channel_id=1, replica_groups=mesh['group'=8,'lat'=2,'rad'=2] {'group','lat','rad'}, use_global_device_ids=true, to_apply=%region_18.19 | all-reduce | flops 2 | bytes 16 | tf_op jit(solution)/shard_map/psum | solution.py:222
  261.7 40.9 %psum.73 = f32[]{:T(128)} all-reduce(f32[]{:T(128)} %multiply_reduce_fusion.4), channel_id=1, replica_groups=mesh['group'=8,'lat'=2,'rad'=2] {'group','lat','rad'}, use_global_device_ids=true, to_apply=%region_22.23 | all-reduce | flops 1 | bytes 8 | tf_op jit(solution)/shard_map/psum | solution.py:222
  305.2 5.0 collective-permute-start.28
  313.0 4.5 collective-permute-start.30
  332.2 43.2 %psum.74 = f32[]{:T(128)} all-reduce(f32[]{:T(128)} %get-tuple-element.399), channel_id=1, replica_groups=mesh['group'=8,'lat'=2,'rad'=2] {'group','lat','rad'}, use_global_device_ids=true, to_apply=%region_24.25 | all-reduce | flops 1 | bytes 8 | tf_op jit(solution)/shard_map/psum | solution.py:230
  377.3 40.4 %psum.75 = f32[]{:T(128)} all-reduce(f32[]{:T(128)} %get-tuple-element.397), channel_id=1, replica_groups=mesh['group'=8,'lat'=2,'rad'=2] {'group','lat','rad'}, use_global_device_ids=true, to_apply=%region_26.27 | all-reduce | flops 1 | bytes 8 | tf_op jit(solution)/shard_map/psum | solution.py:222
  420.4 5.0 collective-permute-start.34
  428.1 4.5 collective-permute-start.36
  447.3 43.4 %psum.76 = f32[]{:T(128)} all-reduce(f32[]{:T(128)} %get-tuple-element.395), channel_id=1, replica_groups=mesh['group'=8,'lat'=2,'rad'=2] {'group','lat','rad'}, use_global_device_ids=true, to_apply=%region_28.29 | all-reduce | flops 1 | bytes 8 | tf_op jit(solution)/shard_map/psum | solution.py:230
  492.7 41.1 %psum.77 = f32[]{:T(128)} all-reduce(f32[]{:T(128)} %multiply_reduce_fusion), channel_id=1, replica_groups=mesh['group'=8,'lat'=2,'rad'=2] {'group','lat','rad'}, use_global_device_ids=true, to_apply=%region_30.31 | all-reduce | flops 1 | bytes 8 | tf_op jit(solution)/shard_map/psum | solution.py:222
  536.5 5.0 collective-permute-start.40
  544.3 4.5 collective-permute-start.42
  563.5 43.2 %psum.78 = f32[]{:T(128)} all-reduce(f32[]{:T(128)} %fusion.707), channel_id=1, replica_groups=mesh['group'=8,'lat'=2,'rad'=2] {'group','lat','rad'}, use_global_device_ids=true, to_apply=%region_32.33 | all-reduce | flops 1 | bytes 8 | tf_op jit(solution)/shard_map/psum | solution.py:230
  609.0 40.8 %psum.79 = f32[64,128]{1,0:T(8,128)S(1)} all-reduce(f32[64,128]{1,0:T(8,128)S(1)} %fusion.711), channel_id=1, replica_groups=mesh['group'=8,'lat'=2,'rad'=2] {'group','lat','rad'}, use_global_device_ids=true, to_apply=%region_34.35 | all-reduce | flops 8192 | bytes 65536 | tf_op jit(solution)/shard_map/psum | solution.py:244
  (212 shorter events, 153.4 us)
Async XLA Ops:
  4.0 41.0 %collective-permute-start.17 = (f32[5,2,1,128]{3,0,2,1:T(8,128)S(1)}, f32[5,2,1,128]{3,0,2,1:T(8,128)S(1)}, u32[]{:S(2)}, u32[]{:S(2)}) collective-permute-start(f32[5,2,1,128]{3,0,2,1:T(8,128)S(1)} %get-tuple-element.513), channel_id=1, source_target_pairs={{4,0},{8,4},{12,8},{16,12},{20,16},{24,20},{28,24},{5,1},{9,5},{13... | collective-permute-start | bytes 15368 | tf_op jit(solution)/shard_map/ppermute | solution.py:33
  5.3 39.7 %collective-permute-start.16 = (f32[5,2,1,128]{3,0,2,1:T(8,128)S(1)}, f32[5,2,1,128]{3,0,2,1:T(8,128)S(1)}, u32[]{:S(2)}, u32[]{:S(2)}) collective-permute-start(f32[5,2,1,128]{3,0,2,1:T(8,128)S(1)} %get-tuple-element.512), channel_id=1, source_target_pairs={{0,4},{4,8},{8,12},{12,16},{16,20},{20,24},{24,28},{1,5},{5,9},{9,... | collective-permute-start | bytes 15368 | tf_op jit(solution)/shard_map/ppermute | solution.py:31
  11.8 14.8 %collective-permute-start.1 = (f32[16,1,256]{2,1,0:T(1,128)S(1)}, f32[16,1,256]{2,1,0:T(1,128)S(1)}, u32[]{:S(2)}, u32[]{:S(2)}) collective-permute-start(f32[16,1,256]{2,1,0:T(1,128)S(1)} %get-tuple-element.461), channel_id=1, source_target_pairs={{2,0},{3,1},{6,4},{7,5},{10,8},{11,9},{14,12},{15,13},{18,16},{19,... | collective-permute-start | bytes 49160 | tf_op jit(solution)/shard_map/ppermute | solution.py:33
  13.8 7.4 %collective-permute-start.3 = (f32[1,256]{1,0:T(1,128)S(1)}, f32[1,256]{1,0:T(1,128)S(1)}, u32[]{:S(2)}, u32[]{:S(2)}) collective-permute-start(f32[1,256]{1,0:T(1,128)S(1)} %get-tuple-element.533), channel_id=1, source_target_pairs={{0,2},{1,3},{4,6},{5,7},{8,10},{9,11},{12,14},{13,15},{16,18},{17,... | collective-permute-start | bytes 3080 | tf_op jit(solution)/shard_map/ppermute | solution.py:31
  18.4 7.4 %collective-permute-start.2 = (f32[1,256]{1,0:T(1,128)S(1)}, f32[1,256]{1,0:T(1,128)S(1)}, u32[]{:S(2)}, u32[]{:S(2)}) collective-permute-start(f32[1,256]{1,0:T(1,128)S(1)} %get-tuple-element.532), channel_id=1, source_target_pairs={{2,0},{3,1},{6,4},{7,5},{10,8},{11,9},{14,12},{15,13},{18,16},{19,... | collective-permute-start | bytes 3080 | tf_op jit(solution)/shard_map/ppermute | solution.py:33
  29.3 7.8 %collective-permute-start.5 = (f32[16,1,256]{2,1,0:T(1,128)S(1)}, f32[16,1,256]{2,1,0:T(1,128)S(1)}, u32[]{:S(2)}, u32[]{:S(2)}) collective-permute-start(f32[16,1,256]{2,1,0:T(1,128)S(1)} %get-tuple-element.459), channel_id=1, source_target_pairs={{2,0},{3,1},{6,4},{7,5},{10,8},{11,9},{14,12},{15,13},{18,16},{19,... | collective-permute-start | bytes 49160 | tf_op jit(solution)/shard_map/ppermute | solution.py:33
  30.6 6.5 %collective-permute-start.4 = (f32[16,1,256]{2,1,0:T(1,128)S(1)}, f32[16,1,256]{2,1,0:T(1,128)S(1)}, u32[]{:S(2)}, u32[]{:S(2)}) collective-permute-start(f32[16,1,256]{2,1,0:T(1,128)S(1)} %get-tuple-element.458), channel_id=1, source_target_pairs={{0,2},{1,3},{4,6},{5,7},{8,10},{9,11},{12,14},{13,15},{16,18},{17,... | collective-permute-start | bytes 49160 | tf_op jit(solution)/shard_map/ppermute | solution.py:31
  48.4 11.8 %collective-permute-start.9 = (f32[16,1,256]{2,1,0:T(1,128)S(1)}, f32[16,1,256]{2,1,0:T(1,128)S(1)}, u32[]{:S(2)}, u32[]{:S(2)}) collective-permute-start(f32[16,1,256]{2,1,0:T(1,128)S(1)} %get-tuple-element.455), channel_id=1, source_target_pairs={{2,0},{3,1},{6,4},{7,5},{10,8},{11,9},{14,12},{15,13},{18,16},{19,... | collective-permute-start | bytes 49160 | tf_op jit(solution)/shard_map/ppermute | solution.py:33
  49.7 10.5 %collective-permute-start.8 = (f32[16,1,256]{2,1,0:T(1,128)S(1)}, f32[16,1,256]{2,1,0:T(1,128)S(1)}, u32[]{:S(2)}, u32[]{:S(2)}) collective-permute-start(f32[16,1,256]{2,1,0:T(1,128)S(1)} %get-tuple-element.454), channel_id=1, source_target_pairs={{0,2},{1,3},{4,6},{5,7},{8,10},{9,11},{12,14},{13,15},{16,18},{17,... | collective-permute-start | bytes 49160 | tf_op jit(solution)/shard_map/ppermute | solution.py:31
  54.4 13.8 %collective-permute-start.19 = (f32[5,2,18,1]{3,0,2,1:T(8,128)S(1)}, f32[5,2,18,1]{3,0,2,1:T(8,128)S(1)}, u32[]{:S(2)}, u32[]{:S(2)}) collective-permute-start(f32[5,2,18,1]{3,0,2,1:T(8,128)S(1)} %get-tuple-element.511), channel_id=1, source_target_pairs={{2,0},{3,1},{6,4},{7,5},{10,8},{11,9},{14,12},{15,13},{18,16},{19,... | collective-permute-start | bytes 2168 | tf_op jit(solution)/shard_map/ppermute | solution.py:33
  55.7 12.5 %collective-permute-start.18 = (f32[5,2,18,1]{3,0,2,1:T(8,128)S(1)}, f32[5,2,18,1]{3,0,2,1:T(8,128)S(1)}, u32[]{:S(2)}, u32[]{:S(2)}) collective-permute-start(f32[5,2,18,1]{3,0,2,1:T(8,128)S(1)} %get-tuple-element.510), channel_id=1, source_target_pairs={{0,2},{1,3},{4,6},{5,7},{8,10},{9,11},{12,14},{13,15},{16,18},{17,... | collective-permute-start | bytes 2168 | tf_op jit(solution)/shard_map/ppermute | solution.py:31
  71.6 10.2 %collective-permute-start.13 = (f32[16,1,256]{2,1,0:T(1,128)S(1)}, f32[16,1,256]{2,1,0:T(1,128)S(1)}, u32[]{:S(2)}, u32[]{:S(2)}) collective-permute-start(f32[16,1,256]{2,1,0:T(1,128)S(1)} %get-tuple-element.451), channel_id=1, source_target_pairs={{2,0},{3,1},{6,4},{7,5},{10,8},{11,9},{14,12},{15,13},{18,16},{19,... | collective-permute-start | bytes 49160 | tf_op jit(solution)/shard_map/ppermute | solution.py:33
  72.9 8.9 %collective-permute-start.12 = (f32[16,1,256]{2,1,0:T(1,128)S(1)}, f32[16,1,256]{2,1,0:T(1,128)S(1)}, u32[]{:S(2)}, u32[]{:S(2)}) collective-permute-start(f32[16,1,256]{2,1,0:T(1,128)S(1)} %get-tuple-element.450), channel_id=1, source_target_pairs={{0,2},{1,3},{4,6},{5,7},{8,10},{9,11},{12,14},{13,15},{16,18},{17,... | collective-permute-start | bytes 49160 | tf_op jit(solution)/shard_map/ppermute | solution.py:31
  77.5 11.5 %collective-permute-start.21 = (f32[5,1,18,130]{3,0,2,1:T(8,128)S(1)}, f32[5,1,18,130]{3,0,2,1:T(8,128)S(1)}, u32[]{:S(2)}, u32[]{:S(2)}) collective-permute-start(f32[5,1,18,130]{3,0,2,1:T(8,128)S(1)} %get-tuple-element.449), channel_id=1, source_target_pairs={{1,0},{3,2},{5,4},{7,6},{9,8},{11,10},{13,12},{15,14},{17,16},{19,... | collective-permute-start | bytes 140408 | tf_op jit(solution)/shard_map/ppermute | solution.py:33
  78.8 10.2 %collective-permute-start.20 = (f32[5,1,18,130]{3,0,2,1:T(8,128)S(1)}, f32[5,1,18,130]{3,0,2,1:T(8,128)S(1)}, u32[]{:S(2)}, u32[]{:S(2)}) collective-permute-start(f32[5,1,18,130]{3,0,2,1:T(8,128)S(1)} %get-tuple-element.448), channel_id=1, source_target_pairs={{0,1},{2,3},{4,5},{6,7},{8,9},{10,11},{12,13},{14,15},{16,17},{18,... | collective-permute-start | bytes 140408 | tf_op jit(solution)/shard_map/ppermute | solution.py:31
  85.8 11.4 %collective-permute-start.15 = (f32[1,256]{1,0:T(1,128)}, f32[1,256]{1,0:T(1,128)}, u32[]{:S(2)}, u32[]{:S(2)}) collective-permute-start(f32[1,256]{1,0:T(1,128)} %get-tuple-element.531), channel_id=1, source_target_pairs={{0,2},{1,3},{4,6},{5,7},{8,10},{9,11},{12,14},{13,15},{16,18},{17,... | collective-permute-start | bytes 3080 | tf_op jit(solution)/shard_map/ppermute | solution.py:31
  87.6 9.6 %collective-permute-start.14 = (f32[1,256]{1,0:T(1,128)}, f32[1,256]{1,0:T(1,128)}, u32[]{:S(2)}, u32[]{:S(2)}) collective-permute-start(f32[1,256]{1,0:T(1,128)} %get-tuple-element.530), channel_id=1, source_target_pairs={{2,0},{3,1},{6,4},{7,5},{10,8},{11,9},{14,12},{15,13},{18,16},{19,... | collective-permute-start | bytes 3080 | tf_op jit(solution)/shard_map/ppermute | solution.py:33
  200.2 6.5 %collective-permute-start.24 = (f32[3,2,18,1]{3,0,2,1:T(4,128)S(1)}, f32[3,2,18,1]{3,0,2,1:T(4,128)S(1)}, u32[]{:S(2)}, u32[]{:S(2)}) collective-permute-start(f32[3,2,18,1]{3,0,2,1:T(4,128)S(1)} %get-tuple-element.520), channel_id=1, source_target_pairs={{0,2},{1,3},{4,6},{5,7},{8,10},{9,11},{12,14},{13,15},{16,18},{17,... | collective-permute-start | bytes 1304 | tf_op jit(solution)/shard_map/ppermute | solution.py:31
  305.2 6.3 collective-permute-start.28
  313.0 6.5 %collective-permute-start.30 = (f32[3,2,18,1]{3,0,2,1:T(4,128)S(1)}, f32[3,2,18,1]{3,0,2,1:T(4,128)S(1)}, u32[]{:S(2)}, u32[]{:S(2)}) collective-permute-start(f32[3,2,18,1]{3,0,2,1:T(4,128)S(1)} %get-tuple-element.518), channel_id=1, source_target_pairs={{0,2},{1,3},{4,6},{5,7},{8,10},{9,11},{12,14},{13,15},{16,18},{17,... | collective-permute-start | bytes 1304 | tf_op jit(solution)/shard_map/ppermute | solution.py:31
  420.4 6.3 collective-permute-start.34
  428.1 6.5 %collective-permute-start.36 = (f32[3,2,18,1]{3,0,2,1:T(4,128)S(1)}, f32[3,2,18,1]{3,0,2,1:T(4,128)S(1)}, u32[]{:S(2)}, u32[]{:S(2)}) collective-permute-start(f32[3,2,18,1]{3,0,2,1:T(4,128)S(1)} %get-tuple-element.516), channel_id=1, source_target_pairs={{0,2},{1,3},{4,6},{5,7},{8,10},{9,11},{12,14},{13,15},{16,18},{17,... | collective-permute-start | bytes 1304 | tf_op jit(solution)/shard_map/ppermute | solution.py:31
  536.5 6.3 collective-permute-start.40
  544.3 6.5 %collective-permute-start.42 = (f32[3,2,18,1]{3,0,2,1:T(4,128)S(1)}, f32[3,2,18,1]{3,0,2,1:T(4,128)S(1)}, u32[]{:S(2)}, u32[]{:S(2)}) collective-permute-start(f32[3,2,18,1]{3,0,2,1:T(4,128)S(1)} %get-tuple-element.514), channel_id=1, source_target_pairs={{0,2},{1,3},{4,6},{5,7},{8,10},{9,11},{12,14},{13,15},{16,18},{17,... | collective-permute-start | bytes 1304 | tf_op jit(solution)/shard_map/ppermute | solution.py:31
  (29 other events, 323.2 us)
where the time goes:
time: 655 us; the launch traced here: 650 us
  blocking collectives  425 us (65%)
  starting transfers between devices  127 us (19%)
  local copies, waits for them, and re-layouts  39.4 us (6%)
  other arithmetic  22.9 us (3%)
  waiting for transfers between devices  18.6 us (3%)
  between operations  11.2 us (2%)
    psum x4, blocking collectives, global_norm(): return lax.psum(jnp.sum(values * values), ('group', 'lat', 'rad'))  163 us
    psum x3, blocking collectives, per_device(): lax.psum(jnp.sum(direction * mapped), ('group', 'lat', 'rad'))  130 us
    ppermute x23, starting transfers between devices, padded(): lax.ppermute(tail, axis, [(i, (i + 1) % count) for i in range(ends)])  97.1 us
    psum x1, blocking collectives, broadcast(): return lax.psum(kept, axis)  87.5 us
    psum x1, blocking collectives, per_device(): lax.psum(jnp.dot(selector, contrib, precision=lax.Precision.HIGHEST, pref...  40.8 us
    ppermute x23, starting transfers between devices, padded(): lax.ppermute(head, axis, [((i + 1) % count, i) for i in range(ends)])  29.7 us
    concatenate x5, local copies, waits for them, and re-layouts, element_apply(): stacked = jnp.concatenate(pieces, 0)  21.6 us
    ppermute x23, waiting for transfers between devices, padded(): lax.ppermute(tail, axis, [(i, (i + 1) % count) for i in range(ends)])  17.1 us
  transfers between devices with their start and end apart: 46, of which 19 were waited for; matrix products, arithmetic and copies ran while one was open for 4% of the time, Pallas kernels for 0%

commit v1 on v0

--- a/solution.py
+++ b/solution.py
@@ -241,11 +241,11 @@
         jnp.int32, (tile_height * lax.axis_size("lat"), flat_index.shape[0]), 0
     )
     selector = (targets == flat_index[None, :]).astype(jnp.float32)
-    all_lift = lax.psum(
+    attach_indices = lambda block_in: lax.psum(lax.psum(block_in, ("lat", "rad")), "group")
+    all_lift = attach_indices(
         jnp.dot(
             selector, contrib, precision=lax.Precision.HIGHEST, preferred_element_type=jnp.float32
-        ),
-        ("group", "lat", "rad"),
+        )
     )
     own_lift = lax.dynamic_slice_in_dim(
         all_lift, lax.axis_index("lat") * tile_height, tile_height, 0

time: 655 us -> 660 us (level)
    psum x1 -> x2, blocking collectives: 40.8 us -> 46.8 us  [the longest x1 35.3 us: per_device(): lax.psum(lax.psum(block_in, ('lat', 'rad')), 'group')]
where the time goes in v1:
time: 660 us; the launch traced here: 656 us
  blocking collectives  431 us (65%)
  starting transfers between devices  127 us (19%)
  local copies, waits for them, and re-layouts  39.4 us (6%)
  other arithmetic  22.9 us (3%)
  waiting for transfers between devices  18.6 us (3%)
  between operations  11.2 us (2%)
    psum x4, blocking collectives, global_norm(): return lax.psum(jnp.sum(values * values), ('group', 'lat', 'rad'))  163 us
    psum x3, blocking collectives, per_device(): lax.psum(jnp.sum(direction * mapped), ('group', 'lat', 'rad'))  130 us
    ppermute x23, starting transfers between devices, padded(): lax.ppermute(tail, axis, [(i, (i + 1) % count) for i in range(ends)])  97.1 us
    psum x1, blocking collectives, broadcast(): return lax.psum(kept, axis)  87.3 us
    psum x1, blocking collectives, per_device(): lax.psum(lax.psum(block_in, ('lat', 'rad')), 'group')  35.3 us
    ppermute x23, starting transfers between devices, padded(): lax.ppermute(head, axis, [((i + 1) % count, i) for i in range(ends)])  29.7 us
    concatenate x5, local copies, waits for them, and re-layouts, element_apply(): stacked = jnp.concatenate(pieces, 0)  21.6 us
    ppermute x23, waiting for transfers between devices, padded(): lax.ppermute(tail, axis, [(i, (i + 1) % count) for i in range(ends)])  17.1 us
  transfers between devices with their start and end apart: 46, of which 19 were waited for; matrix products, arithmetic and copies ran while one was open for 4% of the time, Pallas kernels for 0%

profile of v1, /device:TPU:0, one launch (start us, length us, event | category | flops | bytes accessed | tf_op | source)
XLA Modules:
  0.0 656.2 jit_solution(9583999807098391568)
XLA Ops:
  5.3 5.5 collective-permute-start.16
  30.6 4.5 collective-permute-start.4
  40.4 4.5 collective-permute-start.6
  55.7 4.6 collective-permute-start.18
  63.6 4.5 collective-permute-start.10
  89.9 7.3 %conditional.13 = (f32[3,2,16,128]{3,0,2,1:T(4,128)S(1)}) conditional(s32[]{:T(128)} %convert_element_type.28, (f32[5,4,18,130]{3,0,2,1:T(8,128)S(1)}, f32[24,24]{1,0:T(8,128)S(1)}, f32[3,17,129]{2,0,1:T(4,128)}, f32[]{:T(128)}) %tuple.375, () %tuple.72), branch_computations={%region_15.16_spmd, %region_16.17_spmd} | conditional | flops 45782880 | bytes 5078236 | solution.py:205
  98.1 87.3 %psum.77 = bf16[16,256]{1,0:T(8,128)(2,1)S(1)} all-reduce(bf16[16,256]{1,0:T(8,128)(2,1)S(1)} %select_select_fusion), channel_id=1, replica_groups=mesh['group'=8,'lat'=2,'rad'=2] {'group'}, use_global_device_ids=true, to_apply=%region_13.14 | all-reduce | flops 4096 | bytes 16384 | tf_op jit(solution)/shard_map/psum | solution.py:42
  192.7 4.5 collective-permute-start.22
  200.0 4.5 collective-permute-start.24
  219.1 40.3 %all-reduce.13 = (f32[]{:T(128)}, f32[]{:T(128)}) all-reduce(f32[]{:T(128)} %get-tuple-element.190, f32[]{:T(128)} %get-tuple-element.189), channel_id=1, replica_groups=mesh['group'=8,'lat'=2,'rad'=2] {'group','lat','rad'}, use_global_device_ids=true, to_apply=%region_18.19 | all-reduce | flops 2 | bytes 16 | tf_op jit(solution)/shard_map/psum | solution.py:222
  261.4 40.9 %psum.80 = f32[]{:T(128)} all-reduce(f32[]{:T(128)} %multiply_reduce_fusion.4), channel_id=1, replica_groups=mesh['group'=8,'lat'=2,'rad'=2] {'group','lat','rad'}, use_global_device_ids=true, to_apply=%region_22.23 | all-reduce | flops 1 | bytes 8 | tf_op jit(solution)/shard_map/psum | solution.py:222
  305.0 5.0 collective-permute-start.28
  312.8 4.5 collective-permute-start.30
  331.9 43.2 %psum.81 = f32[]{:T(128)} all-reduce(f32[]{:T(128)} %get-tuple-element.399), channel_id=1, replica_groups=mesh['group'=8,'lat'=2,'rad'=2] {'group','lat','rad'}, use_global_device_ids=true, to_apply=%region_24.25 | all-reduce | flops 1 | bytes 8 | tf_op jit(solution)/shard_map/psum | solution.py:230
  377.1 40.4 %psum.82 = f32[]{:T(128)} all-reduce(f32[]{:T(128)} %get-tuple-element.397), channel_id=1, replica_groups=mesh['group'=8,'lat'=2,'rad'=2] {'group','lat','rad'}, use_global_device_ids=true, to_apply=%region_26.27 | all-reduce | flops 1 | bytes 8 | tf_op jit(solution)/shard_map/psum | solution.py:222
  420.2 5.0 collective-permute-start.34
  427.9 4.5 collective-permute-start.36
  447.1 43.4 %psum.83 = f32[]{:T(128)} all-reduce(f32[]{:T(128)} %get-tuple-element.395), channel_id=1, replica_groups=mesh['group'=8,'lat'=2,'rad'=2] {'group','lat','rad'}, use_global_device_ids=true, to_apply=%region_28.29 | all-reduce | flops 1 | bytes 8 | tf_op jit(solution)/shard_map/psum | solution.py:230
  492.5 41.1 %psum.84 = f32[]{:T(128)} all-reduce(f32[]{:T(128)} %multiply_reduce_fusion), channel_id=1, replica_groups=mesh['group'=8,'lat'=2,'rad'=2] {'group','lat','rad'}, use_global_device_ids=true, to_apply=%region_30.31 | all-reduce | flops 1 | bytes 8 | tf_op jit(solution)/shard_map/psum | solution.py:222
  536.3 5.0 collective-permute-start.40
  544.0 4.5 collective-permute-start.42
  563.3 43.2 %psum.85 = f32[]{:T(128)} all-reduce(f32[]{:T(128)} %fusion.707), channel_id=1, replica_groups=mesh['group'=8,'lat'=2,'rad'=2] {'group','lat','rad'}, use_global_device_ids=true, to_apply=%region_32.33 | all-reduce | flops 1 | bytes 8 | tf_op jit(solution)/shard_map/psum | solution.py:230
  608.8 11.5 %psum.86 = f32[64,128]{1,0:T(8,128)S(1)} all-reduce(f32[64,128]{1,0:T(8,128)S(1)} %fusion.711), channel_id=1, replica_groups=mesh['group'=8,'lat'=2,'rad'=2] {'lat','rad'}, use_global_device_ids=true, to_apply=%region_34.35 | all-reduce | flops 8192 | bytes 65536 | tf_op jit(solution)/shard_map/psum | solution.py:244
  620.3 35.3 %psum.87 = f32[64,128]{1,0:T(8,128)S(1)} all-reduce(f32[64,128]{1,0:T(8,128)S(1)} %psum.86), channel_id=1, replica_groups=mesh['group'=8,'lat'=2,'rad'=2] {'group'}, use_global_device_ids=true, to_apply=%region_35.36 | all-reduce | flops 8192 | bytes 65536 | tf_op jit(solution)/shard_map/psum | solution.py:244
  (213 shorter events, 157.9 us)
Async XLA Ops:
  4.0 41.0 %collective-permute-start.17 = (f32[5,2,1,128]{3,0,2,1:T(8,128)S(1)}, f32[5,2,1,128]{3,0,2,1:T(8,128)S(1)}, u32[]{:S(2)}, u32[]{:S(2)}) collective-permute-start(f32[5,2,1,128]{3,0,2,1:T(8,128)S(1)} %get-tuple-element.513), channel_id=1, source_target_pairs={{4,0},{8,4},{12,8},{16,12},{20,16},{24,20},{28,24},{5,1},{9,5},{13... | collective-permute-start | bytes 15368 | tf_op jit(solution)/shard_map/ppermute | solution.py:33
  5.3 39.7 %collective-permute-start.16 = (f32[5,2,1,128]{3,0,2,1:T(8,128)S(1)}, f32[5,2,1,128]{3,0,2,1:T(8,128)S(1)}, u32[]{:S(2)}, u32[]{:S(2)}) collective-permute-start(f32[5,2,1,128]{3,0,2,1:T(8,128)S(1)} %get-tuple-element.512), channel_id=1, source_target_pairs={{0,4},{4,8},{8,12},{12,16},{16,20},{20,24},{24,28},{1,5},{5,9},{9,... | collective-permute-start | bytes 15368 | tf_op jit(solution)/shard_map/ppermute | solution.py:31
  11.8 14.8 %collective-permute-start.1 = (f32[16,1,256]{2,1,0:T(1,128)S(1)}, f32[16,1,256]{2,1,0:T(1,128)S(1)}, u32[]{:S(2)}, u32[]{:S(2)}) collective-permute-start(f32[16,1,256]{2,1,0:T(1,128)S(1)} %get-tuple-element.461), channel_id=1, source_target_pairs={{2,0},{3,1},{6,4},{7,5},{10,8},{11,9},{14,12},{15,13},{18,16},{19,... | collective-permute-start | bytes 49160 | tf_op jit(solution)/shard_map/ppermute | solution.py:33
  13.8 7.4 %collective-permute-start.3 = (f32[1,256]{1,0:T(1,128)S(1)}, f32[1,256]{1,0:T(1,128)S(1)}, u32[]{:S(2)}, u32[]{:S(2)}) collective-permute-start(f32[1,256]{1,0:T(1,128)S(1)} %get-tuple-element.533), channel_id=1, source_target_pairs={{0,2},{1,3},{4,6},{5,7},{8,10},{9,11},{12,14},{13,15},{16,18},{17,... | collective-permute-start | bytes 3080 | tf_op jit(solution)/shard_map/ppermute | solution.py:31
  18.4 7.4 %collective-permute-start.2 = (f32[1,256]{1,0:T(1,128)S(1)}, f32[1,256]{1,0:T(1,128)S(1)}, u32[]{:S(2)}, u32[]{:S(2)}) collective-permute-start(f32[1,256]{1,0:T(1,128)S(1)} %get-tuple-element.532), channel_id=1, source_target_pairs={{2,0},{3,1},{6,4},{7,5},{10,8},{11,9},{14,12},{15,13},{18,16},{19,... | collective-permute-start | bytes 3080 | tf_op jit(solution)/shard_map/ppermute | solution.py:33
  29.3 7.8 %collective-permute-start.5 = (f32[16,1,256]{2,1,0:T(1,128)S(1)}, f32[16,1,256]{2,1,0:T(1,128)S(1)}, u32[]{:S(2)}, u32[]{:S(2)}) collective-permute-start(f32[16,1,256]{2,1,0:T(1,128)S(1)} %get-tuple-element.459), channel_id=1, source_target_pairs={{2,0},{3,1},{6,4},{7,5},{10,8},{11,9},{14,12},{15,13},{18,16},{19,... | collective-permute-start | bytes 49160 | tf_op jit(solution)/shard_map/ppermute | solution.py:33
  30.6 6.5 collective-permute-start.4
  48.4 11.8 %collective-permute-start.9 = (f32[16,1,256]{2,1,0:T(1,128)S(1)}, f32[16,1,256]{2,1,0:T(1,128)S(1)}, u32[]{:S(2)}, u32[]{:S(2)}) collective-permute-start(f32[16,1,256]{2,1,0:T(1,128)S(1)} %get-tuple-element.455), channel_id=1, source_target_pairs={{2,0},{3,1},{6,4},{7,5},{10,8},{11,9},{14,12},{15,13},{18,16},{19,... | collective-permute-start | bytes 49160 | tf_op jit(solution)/shard_map/ppermute | solution.py:33
  49.7 10.5 %collective-permute-start.8 = (f32[16,1,256]{2,1,0:T(1,128)S(1)}, f32[16,1,256]{2,1,0:T(1,128)S(1)}, u32[]{:S(2)}, u32[]{:S(2)}) collective-permute-start(f32[16,1,256]{2,1,0:T(1,128)S(1)} %get-tuple-element.454), channel_id=1, source_target_pairs={{0,2},{1,3},{4,6},{5,7},{8,10},{9,11},{12,14},{13,15},{16,18},{17,... | collective-permute-start | bytes 49160 | tf_op jit(solution)/shard_map/ppermute | solution.py:31
  54.4 13.8 %collective-permute-start.19 = (f32[5,2,18,1]{3,0,2,1:T(8,128)S(1)}, f32[5,2,18,1]{3,0,2,1:T(8,128)S(1)}, u32[]{:S(2)}, u32[]{:S(2)}) collective-permute-start(f32[5,2,18,1]{3,0,2,1:T(8,128)S(1)} %get-tuple-element.511), channel_id=1, source_target_pairs={{2,0},{3,1},{6,4},{7,5},{10,8},{11,9},{14,12},{15,13},{18,16},{19,... | collective-permute-start | bytes 2168 | tf_op jit(solution)/shard_map/ppermute | solution.py:33
  55.7 12.5 %collective-permute-start.18 = (f32[5,2,18,1]{3,0,2,1:T(8,128)S(1)}, f32[5,2,18,1]{3,0,2,1:T(8,128)S(1)}, u32[]{:S(2)}, u32[]{:S(2)}) collective-permute-start(f32[5,2,18,1]{3,0,2,1:T(8,128)S(1)} %get-tuple-element.510), channel_id=1, source_target_pairs={{0,2},{1,3},{4,6},{5,7},{8,10},{9,11},{12,14},{13,15},{16,18},{17,... | collective-permute-start | bytes 2168 | tf_op jit(solution)/shard_map/ppermute | solution.py:31
  71.6 10.2 %collective-permute-start.13 = (f32[16,1,256]{2,1,0:T(1,128)S(1)}, f32[16,1,256]{2,1,0:T(1,128)S(1)}, u32[]{:S(2)}, u32[]{:S(2)}) collective-permute-start(f32[16,1,256]{2,1,0:T(1,128)S(1)} %get-tuple-element.451), channel_id=1, source_target_pairs={{2,0},{3,1},{6,4},{7,5},{10,8},{11,9},{14,12},{15,13},{18,16},{19,... | collective-permute-start | bytes 49160 | tf_op jit(solution)/shard_map/ppermute | solution.py:33
  72.9 8.9 %collective-permute-start.12 = (f32[16,1,256]{2,1,0:T(1,128)S(1)}, f32[16,1,256]{2,1,0:T(1,128)S(1)}, u32[]{:S(2)}, u32[]{:S(2)}) collective-permute-start(f32[16,1,256]{2,1,0:T(1,128)S(1)} %get-tuple-element.450), channel_id=1, source_target_pairs={{0,2},{1,3},{4,6},{5,7},{8,10},{9,11},{12,14},{13,15},{16,18},{17,... | collective-permute-start | bytes 49160 | tf_op jit(solution)/shard_map/ppermute | solution.py:31
  77.5 11.5 %collective-permute-start.21 = (f32[5,1,18,130]{3,0,2,1:T(8,128)S(1)}, f32[5,1,18,130]{3,0,2,1:T(8,128)S(1)}, u32[]{:S(2)}, u32[]{:S(2)}) collective-permute-start(f32[5,1,18,130]{3,0,2,1:T(8,128)S(1)} %get-tuple-element.449), channel_id=1, source_target_pairs={{1,0},{3,2},{5,4},{7,6},{9,8},{11,10},{13,12},{15,14},{17,16},{19,... | collective-permute-start | bytes 140408 | tf_op jit(solution)/shard_map/ppermute | solution.py:33
  78.8 10.2 %collective-permute-start.20 = (f32[5,1,18,130]{3,0,2,1:T(8,128)S(1)}, f32[5,1,18,130]{3,0,2,1:T(8,128)S(1)}, u32[]{:S(2)}, u32[]{:S(2)}) collective-permute-start(f32[5,1,18,130]{3,0,2,1:T(8,128)S(1)} %get-tuple-element.448), channel_id=1, source_target_pairs={{0,1},{2,3},{4,5},{6,7},{8,9},{10,11},{12,13},{14,15},{16,17},{18,... | collective-permute-start | bytes 140408 | tf_op jit(solution)/shard_map/ppermute | solution.py:31
  85.8 11.4 %collective-permute-start.15 = (f32[1,256]{1,0:T(1,128)}, f32[1,256]{1,0:T(1,128)}, u32[]{:S(2)}, u32[]{:S(2)}) collective-permute-start(f32[1,256]{1,0:T(1,128)} %get-tuple-element.531), channel_id=1, source_target_pairs={{0,2},{1,3},{4,6},{5,7},{8,10},{9,11},{12,14},{13,15},{16,18},{17,... | collective-permute-start | bytes 3080 | tf_op jit(solution)/shard_map/ppermute | solution.py:31
  87.7 9.6 %collective-permute-start.14 = (f32[1,256]{1,0:T(1,128)}, f32[1,256]{1,0:T(1,128)}, u32[]{:S(2)}, u32[]{:S(2)}) collective-permute-start(f32[1,256]{1,0:T(1,128)} %get-tuple-element.530), channel_id=1, source_target_pairs={{2,0},{3,1},{6,4},{7,5},{10,8},{11,9},{14,12},{15,13},{18,16},{19,... | collective-permute-start | bytes 3080 | tf_op jit(solution)/shard_map/ppermute | solution.py:33
  200.0 6.5 collective-permute-start.24
  305.0 6.3 collective-permute-start.28
  312.8 6.5 collective-permute-start.30
  420.2 6.3 collective-permute-start.34
  427.9 6.5 collective-permute-start.36
  536.3 6.3 collective-permute-start.40
  544.0 6.5 collective-permute-start.42
  (29 other events, 329.2 us)
